TPU v7x, 512 devices: a whole 4x4x16 slice. The times are simulated.
512 devices in a mesh: wide: 128 (over z, x, core), narrow: 4 (over y).
Axes of the slice: x: 4, y: 4, z: 16, core: 2. Of those that a mesh axis runs over, the one named last changes fastest.
Arguments:
- tokens_in: bfloat16 [16384, 2560], P('wide', 'narrow'), may hold values from -6 to 6
- norm_gain: bfloat16 [2560], replicated, may hold values from 0.099609375 to 1.8984375
- query_weight: bfloat16 [2560, 2560], P('wide', 'narrow'), may hold values from -0.25 to 0.25
- key_weight: bfloat16 [2560, 640], P('wide', 'narrow'), may hold values from -0.125 to 0.125
- value_weight: bfloat16 [2560, 640], P('wide', 'narrow'), may hold values from -0.5 to 0.5
- out_weight: bfloat16 [2560, 2560], P('wide', 'narrow'), may hold values from -0.125 to 0.125
- cache_keys: bfloat16 [640, 131072], P('narrow', 'wide'), may hold values from -64 to 64
- cache_values: bfloat16 [640, 131072], P('narrow', 'wide'), may hold values from -24 to 24
- cached_len: int32 [32], replicated, may hold values from 1 to 4096, as said below
- append_slot: int32 [32], replicated, may hold values from 0 to 4095
- shard_owner: int32 [32], replicated, may hold values from 0 to 3
Outputs:
- attention_update: bfloat16 [16384, 2560], P('wide', 'narrow')
- appended_keys: bfloat16 [640, 131072], P('narrow', 'wide')
- appended_values: bfloat16 [640, 131072], P('narrow', 'wide')
Inputs may be any that keep to these rules, and one draw needn't show every extreme that they name: `cached_len`: each request's number of cached keys; some request holds 4096.
All inputs are finite; a program needn't handle non-finite values.
Results may differ from a plain program's by a relative error of at most 0.012.
The roundings to bfloat16 on the way count: a program that leaves them out, or rounds other values in their place, can miss the bound.
Values may be sent and summed in bfloat16 or wider, within the bound.
A program may use at most 64 MiB of HBM per device.

v0:
```python
import math
import numpy as np
import jax
import jax.numpy as jnp
from jax import lax
from jax.sharding import Mesh, PartitionSpec as P

HEAD_DIM = 80
WIN = 4096
GROUP_BITS = 2
GROUP = 4
EPSILON = 1e-05
ROPE_BASE = 10000.0
LOWEST = -1e30


def from_partner(block, axis, bit):
    count = lax.psum(1, axis)
    route = []
    for low in range(count):
        high = low | 1 << bit
        if high != low and high < count:
            route += [(low, high), (high, low)]
    return lax.ppermute(block, axis, route)


WIDE = ("z", "x", "c")


def gather_rows(block):
    rows = block.shape[0]
    plane = lax.all_gather(block, ("z", "x"), axis=0, tiled=False)
    both = lax.all_gather(plane, "c", axis=0, tiled=False)
    both = jnp.transpose(both, (1, 0, 2, 3))
    return both.reshape(-1, block.shape[1])


def rms_normed(rows_in, gain):
    values = rows_in.astype(jnp.float32)
    scaling = lax.rsqrt(jnp.mean(values * values, axis=-1, keepdims=True) + EPSILON)
    return (values * scaling * gain.astype(jnp.float32)).astype(jnp.bfloat16)


def rotate(values, positions):
    half_dim = values.shape[-1] // 2
    inverse = ROPE_BASE ** (-(jnp.arange(half_dim, dtype=jnp.float32) * (2.0 / values.shape[-1])))
    angles = positions.astype(jnp.float32)[:, None] * inverse[None, :]
    cos_part = jnp.cos(angles)[:, None, :]
    sin_part = jnp.sin(angles)[:, None, :]
    lower = values[..., :half_dim]
    higher = values[..., half_dim:]
    return jnp.concatenate(
        [lower * cos_part - higher * sin_part, higher * cos_part + lower * sin_part], axis=-1
    )


def ordered(mine, other, upper, along):
    first_half = jnp.where(upper, other, mine)
    second_half = jnp.where(upper, mine, other)
    return jnp.concatenate([first_half, second_half], axis=along)


def empty_state(row_count, groups, repeats):
    return (
        jnp.zeros((row_count, groups, repeats, HEAD_DIM), jnp.float32),
        jnp.full((row_count, groups, repeats), LOWEST, jnp.float32),
        jnp.zeros((row_count, groups, repeats), jnp.float32),
    )


def fold_keys(state, queries, query_pos, keys, values, key_pos, key_ok, widest):
    key_count = keys.shape[1]
    groups = queries.shape[1]
    block = math.gcd(key_count, widest)
    keys_split = keys.reshape(groups, HEAD_DIM, key_count)
    values_split = values.reshape(groups, HEAD_DIM, key_count)
    scale = HEAD_DIM ** (-0.5)

    def step(index, carry):
        accum, top_old, sum_old = carry
        start = index * block
        block_keys = lax.dynamic_slice_in_dim(keys_split, start, block, 2)
        block_values = lax.dynamic_slice_in_dim(values_split, start, block, 2)
        block_pos = lax.dynamic_slice_in_dim(key_pos, start, block, 0)
        block_ok = lax.dynamic_slice_in_dim(key_ok, start, block, 0)
        scores = (
            jnp.einsum("tgrd,gdk->tgrk", queries, block_keys, preferred_element_type=jnp.float32)
            * scale
        )
        allowed = (
            block_ok[None, :]
            & (block_pos[None, :] <= query_pos[:, None])
            & (query_pos[:, None] - block_pos[None, :] < WIN)
        )
        allowed = allowed[:, None, None, :]
        top_new = jnp.maximum(top_old, jnp.max(jnp.where(allowed, scores, LOWEST), axis=-1))
        weights = jnp.where(allowed, jnp.exp(scores - top_new[..., None]), 0.0)
        rescale = jnp.exp(top_old - top_new)
        sum_new = sum_old * rescale + jnp.sum(weights, axis=-1)
        mixed = jnp.einsum(
            "tgrk,gdk->tgrd",
            weights.astype(jnp.bfloat16),
            block_values,
            preferred_element_type=jnp.float32,
        )
        return (accum * rescale[..., None] + mixed, top_new, sum_new)

    return lax.fori_loop(0, key_count // block, step, state)


def shards(
    tokens_in,
    norm_gain,
    query_weight,
    key_weight,
    value_weight,
    out_weight,
    cache_keys,
    cache_values,
    cached_len,
    append_slot,
    shard_owner,
):
    whole = lax.all_gather(tokens_in, "narrow", axis=1, tiled=True)
    normed = rms_normed(whole, norm_gain)
    tok_rows = whole.shape[0]
    query_width = query_weight.shape[1]
    kv_width = key_weight.shape[1]
    local_heads = query_width // HEAD_DIM
    local_groups = kv_width // HEAD_DIM
    repeats = local_heads // local_groups
    columns = normed
    qkv = gather_rows(jnp.concatenate([query_weight, key_weight, value_weight], axis=1))
    qkv_sum = jnp.dot(columns, qkv, preferred_element_type=jnp.float32)
    query_sum = qkv_sum[:, :query_width]
    key_sum = qkv_sum[:, query_width : query_width + kv_width]
    value_sum = qkv_sum[:, query_width + kv_width :]
    position = lax.axis_index(WIDE)
    request = position // GROUP
    place = position % GROUP
    length = cached_len[request]
    offset = append_slot[request]
    owner = shard_owner[request]
    query_pos = length + place * tok_rows + jnp.arange(tok_rows, dtype=jnp.int32)
    queries = rotate(query_sum.reshape(tok_rows, local_heads, HEAD_DIM), query_pos).astype(
        jnp.bfloat16
    )
    queries = queries.reshape(tok_rows, local_groups, repeats, HEAD_DIM)
    new_keys = (
        rotate(key_sum.reshape(tok_rows, local_groups, HEAD_DIM), query_pos)
        .astype(jnp.bfloat16)
        .reshape(tok_rows, kv_width)
    )
    new_values = value_sum.astype(jnp.bfloat16)
    shard_rows = cache_keys.shape[1]
    within = jnp.arange(shard_rows, dtype=jnp.int32)
    cycle_mine = (place - owner) % GROUP * shard_rows + within
    old_keys, old_values = (cache_keys, cache_values)
    for bit in range(GROUP_BITS):
        upper = place // 2**bit % 2 == 1
        other_keys, other_values, other_old_keys, other_old_values = from_partner(
            (new_keys, new_values, old_keys, old_values), WIDE, bit
        )
        new_keys = ordered(new_keys, other_keys, upper, 0)
        new_values = ordered(new_values, other_values, upper, 0)
        old_keys = ordered(old_keys, other_old_keys, upper, 1)
        old_values = ordered(old_values, other_old_values, upper, 1)
    slot_index = jnp.arange(old_keys.shape[1], dtype=jnp.int32)
    cycle = (slot_index // shard_rows - owner) % GROUP * shard_rows + slot_index % shard_rows
    cached_pos = (cycle - offset + length) % WIN
    state = fold_keys(
        empty_state(tok_rows, local_groups, repeats),
        queries,
        query_pos,
        old_keys,
        old_values,
        cached_pos,
        cached_pos < length,
        512,
    )
    key_cols = new_keys.T
    value_cols = new_values.T
    new_count = key_cols.shape[1]
    new_pos = length + jnp.arange(new_count, dtype=jnp.int32)
    state = fold_keys(
        state,
        queries,
        query_pos,
        key_cols,
        value_cols,
        new_pos,
        jnp.ones((new_count,), dtype=bool),
        512,
    )
    accum, top_score, total = state
    attended = (accum / total[..., None]).astype(jnp.bfloat16).reshape(tok_rows, query_width)
    all_heads = lax.all_gather(attended, "narrow", axis=1, tiled=True)
    columns = all_heads
    update = jnp.dot(columns, gather_rows(out_weight), preferred_element_type=jnp.float32).astype(
        jnp.bfloat16
    )
    new_index = (cycle_mine - offset) % WIN
    written = new_index < new_count
    take_rows = jnp.minimum(new_index, new_count - 1)
    put_keys = jnp.where(written[None, :], jnp.take(key_cols, take_rows, axis=1), cache_keys)
    put_values = jnp.where(written[None, :], jnp.take(value_cols, take_rows, axis=1), cache_values)
    return (update, put_keys, put_values)


def solution(mesh):
    devices = mesh.devices
    wide_devices = devices[:, 0]
    xs = sorted({d.coords[0] for d in wide_devices})
    cores = sorted({getattr(d, "core_on_chip", 0) for d in wide_devices})
    n_x, n_c = (len(xs), len(cores))
    n_z = devices.shape[0] // (n_x * n_c)
    fine = Mesh(devices.reshape(n_z, n_x, n_c, devices.shape[1]), ("z", "x", "c", "narrow"))
    rows = P(WIDE, "narrow")
    cols = P("narrow", WIDE)
    in_specs = (rows, P(), rows, rows, rows, rows, cols, cols, P(), P(), P())
    out_specs = (rows, cols, cols)
    return jax.shard_map(shards, mesh=fine, in_specs=in_specs, out_specs=out_specs, check_vma=False)
```

profile of v0, /device:TPU:2, one launch (start us, length us, event | category | flops | bytes accessed | tf_op | source)
XLA Modules:
  0.0 497.3 jit_solution(6493536024206706948)
XLA Ops:
  7.9 1.5 maximum_bitcast_fusion
  9.5 145.7 %all-gather.17.cloned.1.call-done = bf16[64,20,640]{2,1,0:T(8,128)(2,1)} async-done(((bf16[1,20,640]{2,1,0:T(8,128)(2,1)}), bf16[64,20,640]{2,1,0:T(8,128)(2,1)}) %all-gather.17.cloned.1.call-update) | async-done | bytes 1638416 | tf_op jit(solution)/shard_map/all_gather | solution.py:32
  155.2 3.0 copy.36
  158.3 139.7 %all-gather.15.cloned.1.call-done = bf16[64,20,960]{2,1,0:T(8,128)(2,1)} async-done(((bf16[1,20,960]{2,1,0:T(8,128)(2,1)}), bf16[64,20,960]{2,1,0:T(8,128)(2,1)}) %all-gather.15.cloned.1.call-update) | async-done | bytes 2457616 | tf_op jit(solution)/shard_map/all_gather | solution.py:32
  298.0 4.8 copy.33
  303.8 1.9 collective-permute-start.2
  305.7 2.4 collective-permute-start
  314.6 1.9 broadcast_compare_fusion
  317.3 1.9 add_select_fusion
  319.2 13.7 %all_gather.30 = bf16[128,2560]{1,0:T(8,128)(2,1)S(1)} all-gather(bf16[128,640]{1,0:T(8,128)(2,1)S(1)} %copy-done.3), channel_id=1, replica_groups=mesh['z'=16,'x'=4,'c'=2,'narrow'=4] {'narrow'}, dimensions={1}, use_global_device_ids=true | all-gather | bytes 819200 | tf_op jit(solution)/shard_map/all_gather | solution.py:124
  333.4 4.1 collective-permute-start.1
  337.7 2.1 collective-permute-start.3
  339.8 13.3 %collective-permute-done.1 = bf16[160,2048]{1,0:T(8,128)(2,1)S(1)} collective-permute-done((bf16[160,2048]{1,0:T(8,128)(2,1)S(1)}, bf16[160,2048]{1,0:T(8,128)(2,1)S(1)}, u32[]{:S(2)}, u32[]{:S(2)}) %collective-permute-start.1) | collective-permute-done | bytes 655392 | tf_op jit(solution)/shard_map/ppermute | solution.py:24
  354.6 10.1 %collective-permute-done.3 = bf16[160,2048]{1,0:T(8,128)(2,1)S(1)} collective-permute-done((bf16[160,2048]{1,0:T(8,128)(2,1)S(1)}, bf16[160,2048]{1,0:T(8,128)(2,1)S(1)}, u32[]{:S(2)}, u32[]{:S(2)}) %collective-permute-start.3) | collective-permute-done | bytes 655392 | tf_op jit(solution)/shard_map/ppermute | solution.py:24
  366.2 5.7 %copy.53 = bf16[2,64,20,640]{3,2,0,1:T(8,128)(2,1)} copy(bf16[2,64,20,640]{3,1,0,2:T(8,128)(2,1)} %bitcast.126) | data formatting | bytes 6553600 | tf_op jit(solution)/shard_map/all_gather | solution.py:33
  371.9 6.1 %reshape.253 = bf16[2560,640]{1,0:T(8,128)(2,1)} reshape(bf16[64,2,20,640]{3,2,1,0:T(8,128)(2,1)} %bitcast.123) | data formatting | bytes 6553600 | tf_op jit(solution)/shard_map/reshape | solution.py:35
  378.0 8.1 %copy.52 = bf16[2,64,20,960]{3,2,0,1:T(8,128)(2,1)} copy(bf16[2,64,20,960]{3,1,0,2:T(8,128)(2,1)} %bitcast.124) | data formatting | bytes 9830400 | tf_op jit(solution)/shard_map/all_gather | solution.py:33
  386.1 9.8 %reshape.246 = bf16[2560,960]{1,0:T(8,128)(2,1)} reshape(bf16[64,2,20,960]{3,2,1,0:T(8,128)(2,1)} %bitcast.122) | data formatting | bytes 9830400 | tf_op jit(solution)/shard_map/reshape | solution.py:35
  395.9 4.6 fusion.38
  400.6 1.9 collective-permute-start.6
  402.6 2.4 collective-permute-start.4
  405.1 39.9 %while.5 = (s32[]{:T(128)}, f32[128,2,4,80]{0,3,2,1:T(8,128)}, f32[128,2,4]{0,2,1:T(4,128)S(1)}, f32[128,2,4]{0,2,1:T(4,128)S(1)}, pred[4096]{0:T(1024)(128)(4,1...) while((s32[]{:T(128)}, f32[128,2,4,80]{0,3,2,1:T(8,128)}, ...), condition=%wide.region_4.5_spmd.clone, body=%wide.region_1.4_spmd.clone.sunk | while | flops 174118016 | bytes 10396435 | solution.py:108
  405.5 1.4 fusion.83
  407.9 1.5 fusion.86
  410.5 1.4 fusion.83
  412.9 1.5 fusion.86
  415.5 1.4 fusion.83
  417.9 1.5 fusion.86
  420.4 1.4 fusion.83
  422.9 1.5 fusion.86
  425.4 1.4 fusion.83
  427.8 1.5 fusion.86
  430.4 1.4 fusion.83
  432.8 1.5 fusion.86
  435.4 1.4 fusion.83
  437.8 1.5 fusion.86
  440.4 1.4 fusion.83
  442.8 1.5 fusion.86
  445.0 3.6 collective-permute-start.7
  448.7 2.4 collective-permute-start.5
  451.4 3.6 collective-permute-done.5
  456.7 14.5 %all_gather.35 = bf16[128,2560]{0,1:T(8,128)(2,1)} all-gather(bf16[128,640]{0,1:T(8,128)(2,1)S(1)} %bitcast.138), channel_id=1, replica_groups=mesh['z'=16,'x'=4,'c'=2,'narrow'=4] {'narrow'}, dimensions={1}, use_global_device_ids=true | all-gather | bytes 819200 | tf_op jit(solution)/shard_map/all_gather | solution.py:197
  471.4 5.0 %gather_fusion.1 = bf16[1024,160]{1,0:T(8,128)(2,1)} fusion(bf16[160,512]{0,1:T(8,128)(2,1)S(1)} %copy.40, s32[1024]{0:T(1024)S(1)} %fusion.58), kind=kCustom, calls=%fused_computation.1.clone | custom fusion | bytes 659456 | tf_op jit(solution)/shard_map/jit(_take)/gather | solution.py:206
  476.4 5.0 %gather_fusion = bf16[1024,160]{1,0:T(8,128)(2,1)} fusion(bf16[160,512]{0,1:T(8,128)(2,1)S(1)} %copy.38, s32[1024]{0:T(1024)S(1)} %fusion.58), kind=kCustom, calls=%fused_computation.clone | custom fusion | bytes 659456 | tf_op jit(solution)/shard_map/jit(_take)/gather | solution.py:205
  481.4 3.0 bitcast_select_fusion.2
  484.4 1.9 copy.42
  486.3 1.9 copy.43
  488.3 2.5 convolution_convert_fusion
  (176 shorter events, 29.9 us)
Async XLA Ops:
  7.2 148.1 %all-gather.17.cloned.1.call-start = ((), (), s32[]{:S(2)}) async-start(), calls=%async_computation.3 | async-start | bytes 1996800 | tf_op jit(solution)/shard_map/all_gather | solution.py:32
  7.9 290.1 %all-gather.15.cloned.1.call-start = ((), (), s32[]{:S(2)}) async-start(), calls=%async_computation.2 | async-start | bytes 3194880 | tf_op jit(solution)/shard_map/all_gather | solution.py:32
  9.5 356.8 %all-gather.13.cloned.1.call-start = ((), (), s32[]{:S(2)}) async-start(), calls=%async_computation.1 | async-start | bytes 4915200 | tf_op jit(solution)/shard_map/all_gather | solution.py:33
  158.2 219.8 %all-gather.11.cloned.1.call-start = ((), (), s32[]{:S(2)}) async-start(), calls=%async_computation | async-start | bytes 7864320 | tf_op jit(solution)/shard_map/all_gather | solution.py:33
  302.8 1.0 copy-start.1
  302.8 2.9 copy-start.2
  302.8 6.4 %copy-start.5 = (s32[32]{0:T(128)S(1)}, s32[32]{0:T(128)}, u32[]{:S(2)}) copy-start(s32[32]{0:T(128)} %param.25) | copy-start | bytes 388
  302.8 8.5 %copy-start.4 = (bf16[2560]{0:T(1024)(128)(2,1)S(1)}, bf16[2560]{0:T(1024)(128)(2,1)}, u32[]{:S(2)}) copy-start(bf16[2560]{0:T(1024)(128)(2,1)} %param.16) | copy-start | bytes 15364
  302.8 8.5 %copy-start.6 = (s32[32]{0:T(128)S(1)}, s32[32]{0:T(128)}, u32[]{:S(2)}) copy-start(s32[32]{0:T(128)} %param.23) | copy-start | bytes 388
  302.8 9.1 %copy-start.7 = (s32[32]{0:T(128)S(1)}, s32[32]{0:T(128)}, u32[]{:S(2)}) copy-start(s32[32]{0:T(128)} %param.24) | copy-start | bytes 388
  302.8 16.4 %copy-start.3 = (bf16[128,640]{1,0:T(8,128)(2,1)S(1)}, bf16[128,640]{1,0:T(8,128)(2,1)}, u32[]{:S(2)}) copy-start(bf16[128,640]{1,0:T(8,128)(2,1)} %param.15) | copy-start | bytes 491524
  303.8 29.5 %collective-permute-start.2 = (bf16[160,1024]{1,0:T(8,128)(2,1)S(1)}, bf16[160,1024]{1,0:T(8,128)(2,1)S(1)}, u32[]{:S(2)}, u32[]{:S(2)}) collective-permute-start(bf16[160,1024]{1,0:T(8,128)(2,1)S(1)} %copy-done.1), channel_id=1, source_target_pairs={{0,4},{4,0},{8,12},{12,8},{16,20},{20,16},{24,28},{28,24},{32,36},... | collective-permute-start | bytes 983048 | tf_op jit(solution)/shard_map/ppermute | solution.py:24
  305.7 27.6 %collective-permute-start = (bf16[160,1024]{1,0:T(8,128)(2,1)S(1)}, bf16[160,1024]{1,0:T(8,128)(2,1)S(1)}, u32[]{:S(2)}, u32[]{:S(2)}) collective-permute-start(bf16[160,1024]{1,0:T(8,128)(2,1)S(1)} %copy-done.2), channel_id=1, source_target_pairs={{0,4},{4,0},{8,12},{12,8},{16,20},{20,16},{24,28},{28,24},{32,36},... | collective-permute-start | bytes 983048 | tf_op jit(solution)/shard_map/ppermute | solution.py:24
  333.4 19.7 %collective-permute-start.1 = (bf16[160,2048]{1,0:T(8,128)(2,1)S(1)}, bf16[160,2048]{1,0:T(8,128)(2,1)S(1)}, u32[]{:S(2)}, u32[]{:S(2)}) collective-permute-start(bf16[160,2048]{1,0:T(8,128)(2,1)S(1)} %pad_maximum_fusion.2), channel_id=1, source_target_pairs={{0,8},{8,0},{4,12},{12,4},{16,24},{24,16},{20,28},{28,20},{32,40},... | collective-permute-start | bytes 1966088 | tf_op jit(solution)/shard_map/ppermute | solution.py:24
  337.7 27.1 %collective-permute-start.3 = (bf16[160,2048]{1,0:T(8,128)(2,1)S(1)}, bf16[160,2048]{1,0:T(8,128)(2,1)S(1)}, u32[]{:S(2)}, u32[]{:S(2)}) collective-permute-start(bf16[160,2048]{1,0:T(8,128)(2,1)S(1)} %pad_maximum_fusion.3), channel_id=1, source_target_pairs={{0,8},{8,0},{4,12},{12,4},{16,24},{24,16},{20,28},{28,20},{32,40},... | collective-permute-start | bytes 1966088 | tf_op jit(solution)/shard_map/ppermute | solution.py:24
  400.6 44.3 %collective-permute-start.6 = (bf16[128,160]{0,1:T(8,128)(2,1)S(1)}, bf16[128,160]{0,1:T(8,128)(2,1)S(1)}, u32[]{:S(2)}, u32[]{:S(2)}) collective-permute-start(bf16[128,160]{0,1:T(8,128)(2,1)S(1)} %slice.49), channel_id=1, source_target_pairs={{0,4},{4,0},{8,12},{12,8},{16,20},{20,16},{24,28},{28,24},{32,36},... | collective-permute-start | bytes 122888 | tf_op jit(solution)/shard_map/ppermute | solution.py:24
  402.6 42.4 %collective-permute-start.4 = (bf16[128,160]{0,1:T(8,128)(2,1)S(1)}, bf16[128,160]{0,1:T(8,128)(2,1)S(1)}, u32[]{:S(2)}, u32[]{:S(2)}) collective-permute-start(bf16[128,160]{0,1:T(8,128)(2,1)S(1)} %bitcast.136), channel_id=1, source_target_pairs={{0,4},{4,0},{8,12},{12,8},{16,20},{20,16},{24,28},{28,24},{32,36},... | collective-permute-start | bytes 122888 | tf_op jit(solution)/shard_map/ppermute | solution.py:24
  406.9 1.0 copy-start.8
  409.4 0.7 copy-start.9
  411.9 1.0 copy-start.8
  414.4 0.7 copy-start.9
  416.9 1.0 copy-start.8
  419.3 0.7 copy-start.9
  421.9 1.0 copy-start.8
  424.3 0.7 copy-start.9
  426.9 1.0 copy-start.8
  429.3 0.7 copy-start.9
  431.8 1.0 copy-start.8
  434.3 0.7 copy-start.9
  436.8 1.0 copy-start.8
  439.3 0.7 copy-start.9
  441.8 1.0 copy-start.8
  444.2 0.7 copy-start.9
  445.0 6.3 %collective-permute-start.7 = (bf16[256,160]{0,1:T(8,128)(2,1)S(1)}, bf16[256,160]{0,1:T(8,128)(2,1)S(1)}, u32[]{:S(2)}, u32[]{:S(2)}) collective-permute-start(bf16[256,160]{0,1:T(8,128)(2,1)S(1)} %pad_maximum_fusion.8), channel_id=1, source_target_pairs={{0,8},{8,0},{4,12},{12,4},{16,24},{24,16},{20,28},{28,20},{32,40},... | collective-permute-start | bytes 245768 | tf_op jit(solution)/shard_map/ppermute | solution.py:24
  448.7 6.3 %collective-permute-start.5 = (bf16[256,160]{0,1:T(8,128)(2,1)S(1)}, bf16[256,160]{0,1:T(8,128)(2,1)S(1)}, u32[]{:S(2)}, u32[]{:S(2)}) collective-permute-start(bf16[256,160]{0,1:T(8,128)(2,1)S(1)} %pad_maximum_fusion.7), channel_id=1, source_target_pairs={{0,8},{8,0},{4,12},{12,4},{16,24},{24,16},{20,28},{28,20},{32,40},... | collective-permute-start | bytes 245768 | tf_op jit(solution)/shard_map/ppermute | solution.py:24
  455.1 1.0 copy-start.10
  481.4 6.9 %copy-start = (bf16[2560,640]{1,0:T(8,128)(2,1)S(1)}, bf16[2560,640]{1,0:T(8,128)(2,1)}, u32[]{:S(2)}) copy-start(bf16[2560,640]{1,0:T(8,128)(2,1)} %reshape.253) | copy-start | bytes 9830404
Sparse Core Ops, SparseCore 0:
  11.0 144.2 all-gather.16
  158.7 139.1 all-gather.14
  300.1 18.8 all-gather.12
  320.9 27.0 all-gather.10
where the time goes:
time: 499 us; the launch traced here: 497 us
  waiting for transfers between devices  313 us (63%)
  local copies, waits for them, and re-layouts  67.2 us (13%)
  matrix products  31.3 us (6%)
  blocking collectives  28.1 us (6%)
  starting transfers between devices  21 us (4%)
  other arithmetic  20.2 us (4%)
  between operations  15.5 us (3%)
    all_gather x2, waiting for transfers between devices, gather_rows(): plane = lax.all_gather(block, ('z', 'x'), axis=0, tiled=False)  285 us
    ppermute x8, waiting for transfers between devices, from_partner(): return lax.ppermute(block, axis, route)  27.3 us
    ppermute x8, starting transfers between devices, from_partner(): return lax.ppermute(block, axis, route)  20.9 us
    reshape x2, local copies, waits for them, and re-layouts, gather_rows(): return both.reshape(-1, block.shape[1])  15.9 us
    all_gather x1, blocking collectives, shards(): all_heads = lax.all_gather(attended, 'narrow', axis=1, tiled=True)  14.5 us
    all_gather x2, local copies, waits for them, and re-layouts, gather_rows(): both = lax.all_gather(plane, 'c', axis=0, tiled=False)  13.8 us
    all_gather x1, blocking collectives, shards(): whole = lax.all_gather(tokens_in, 'narrow', axis=1, tiled=True)  13.7 us
    dot_general x9, matrix products, step(): jnp.einsum('tgrk,gdk->tgrd', weights.astype(jnp.bfloat16), block_values,...  12.2 us
  transfers between devices with their start and end apart: 12, of which 6 were waited for; matrix products, arithmetic and copies ran while one was open for 13% of the time, Pallas kernels for 0%

commit v1 on v0

--- a/solution.py
+++ b/solution.py
@@ -194,7 +194,8 @@
     )
     accum, top_score, total = state
     attended = (accum / total[..., None]).astype(jnp.bfloat16).reshape(tok_rows, query_width)
-    all_heads = lax.all_gather(attended, "narrow", axis=1, tiled=True)
+    z1 = jnp.concatenate([attended for _ in range(jax.lax.axis_size("narrow"))], 1)
+    all_heads = jax.lax.all_to_all(z1, "narrow", 1, 1, tiled=True)
     columns = all_heads
     update = jnp.dot(columns, gather_rows(out_weight), preferred_element_type=jnp.float32).astype(
         jnp.bfloat16

time: 499 us -> 450 us (0.902)
  the two profiles are of different devices: /device:TPU:2 before, /device:TPU:10 now
where the time goes in v1:
time: 450 us; the launch traced here: 448 us
  waiting for transfers between devices  268 us (60%)
  local copies, waits for them, and re-layouts  70.5 us (16%)
  matrix products  31.6 us (7%)
  starting transfers between devices  26.8 us (6%)
  other arithmetic  20.2 us (4%)
  between operations  15.6 us (3%)
  blocking collectives  14.3 us (3%)
    all_gather x2, waiting for transfers between devices, gather_rows(): plane = lax.all_gather(block, ('z', 'x'), axis=0, tiled=False)  222 us
    ppermute x8, waiting for transfers between devices, from_partner(): return lax.ppermute(block, axis, route)  24.2 us
    all_gather x2, waiting for transfers between devices, gather_rows(): both = lax.all_gather(plane, 'c', axis=0, tiled=False)  21.7 us
    ppermute x8, starting transfers between devices, from_partner(): return lax.ppermute(block, axis, route)  20.6 us
    reshape x2, local copies, waits for them, and re-layouts, gather_rows(): return both.reshape(-1, block.shape[1])  15.9 us
    all_gather x1, blocking collectives, shards(): whole = lax.all_gather(tokens_in, 'narrow', axis=1, tiled=True)  14.3 us
    all_gather x2, local copies, waits for them, and re-layouts, gather_rows(): both = lax.all_gather(plane, 'c', axis=0, tiled=False)  13.9 us
    dot_general x9, matrix products, step(): jnp.einsum('tgrk,gdk->tgrd', weights.astype(jnp.bfloat16), block_values,...  12.2 us
  transfers between devices with their start and end apart: 13, of which 7 were waited for; matrix products, arithmetic and copies ran while one was open for 24% of the time, Pallas kernels for 0%

profile of v1, /device:TPU:10, one launch (start us, length us, event | category | flops | bytes accessed | tf_op | source)
XLA Modules:
  0.0 447.6 jit_solution(8138348600503686866)
XLA Ops:
  7.2 1.5 maximum_bitcast_fusion
  9.5 148.7 %all-gather.15.cloned.1.call-done = bf16[64,20,960]{2,1,0:T(8,128)(2,1)} async-done(((bf16[1,20,960]{2,1,0:T(8,128)(2,1)}), bf16[64,20,960]{2,1,0:T(8,128)(2,1)}) %all-gather.15.cloned.1.call-update) | async-done | bytes 2457616 | tf_op jit(solution)/shard_map/all_gather | solution.py:32
  158.3 4.8 %copy.48 = bf16[64,20,960]{2,0,1:T(8,128)(2,1)} copy(bf16[64,20,960]{2,1,0:T(8,128)(2,1)} %all-gather.15.cloned.1.call-done) | data formatting | bytes 4915200 | tf_op jit(solution)/shard_map/all_gather | solution.py:32
  164.1 1.9 collective-permute-start.2
  166.0 2.4 collective-permute-start
  174.4 2.0 broadcast_compare_fusion
  176.4 2.0 add_select_fusion
  178.4 14.3 %all_gather.27 = bf16[128,2560]{1,0:T(8,128)(2,1)S(1)} all-gather(bf16[128,640]{1,0:T(8,128)(2,1)S(1)} %copy-done.3), channel_id=1, replica_groups=mesh['z'=16,'x'=4,'c'=2,'narrow'=4] {'narrow'}, dimensions={1}, use_global_device_ids=true | all-gather | bytes 819200 | tf_op jit(solution)/shard_map/all_gather | solution.py:124
  193.3 4.1 collective-permute-start.1
  197.5 1.9 collective-permute-start.3
  199.5 13.5 %collective-permute-done.1 = bf16[160,2048]{1,0:T(8,128)(2,1)S(1)} collective-permute-done((bf16[160,2048]{1,0:T(8,128)(2,1)S(1)}, bf16[160,2048]{1,0:T(8,128)(2,1)S(1)}, u32[]{:S(2)}, u32[]{:S(2)}) %collective-permute-start.1) | collective-permute-done | bytes 655392 | tf_op jit(solution)/shard_map/ppermute | solution.py:24
  214.5 8.4 %collective-permute-done.3 = bf16[160,2048]{1,0:T(8,128)(2,1)S(1)} collective-permute-done((bf16[160,2048]{1,0:T(8,128)(2,1)S(1)}, bf16[160,2048]{1,0:T(8,128)(2,1)S(1)}, u32[]{:S(2)}, u32[]{:S(2)}) %collective-permute-start.3) | collective-permute-done | bytes 655392 | tf_op jit(solution)/shard_map/ppermute | solution.py:24
  224.3 72.8 %all-gather.17.cloned.1.call-done = bf16[64,20,640]{2,1,0:T(8,128)(2,1)} async-done(((bf16[1,20,640]{2,1,0:T(8,128)(2,1)}), bf16[64,20,640]{2,1,0:T(8,128)(2,1)}) %all-gather.17.cloned.1.call-update) | async-done | bytes 1638416 | tf_op jit(solution)/shard_map/all_gather | solution.py:32
  297.1 3.0 copy.53
  300.1 21.6 %all-gather.11.cloned.1.call-done = bf16[128,20,960]{2,0,1:T(8,128)(2,1)} async-done(((bf16[64,20,960]{2,0,1:T(8,128)(2,1)}), bf16[128,20,960]{2,0,1:T(8,128)(2,1)}) %all-gather.11.cloned.1.call-update) | async-done | bytes 4915216 | tf_op jit(solution)/shard_map/all_gather | solution.py:33
  321.7 8.1 %copy.69 = bf16[2,64,20,960]{3,2,0,1:T(8,128)(2,1)} copy(bf16[2,64,20,960]{3,1,0,2:T(8,128)(2,1)} %bitcast.125) | data formatting | bytes 9830400 | tf_op jit(solution)/shard_map/all_gather | solution.py:33
  329.9 9.8 %reshape.256 = bf16[2560,960]{1,0:T(8,128)(2,1)} reshape(bf16[64,2,20,960]{3,2,1,0:T(8,128)(2,1)} %bitcast.123) | data formatting | bytes 9830400 | tf_op jit(solution)/shard_map/reshape | solution.py:35
  339.6 5.0 %fusion.38 = f32[128,960]{0,1:T(8,128)S(1)} fusion(bf16[2560,960]{1,0:T(8,128)(2,1)} %reshape.256, bf16[128,2560]{1,0:T(8,128)(2,1)S(1)} %all_gather.27, f32[2560]{0:T(1024)S(1)} %convert_element_type.43, f32[128]{0:T(128)S(1)} %add_rsqrt_fusion), kind=kOutput, calls=%fused_computation.56 | convolution fusion | flops 630456320 | bytes 6072832 | tf_op jit(solution)/shard_map/dot_general | solution.py:134
  344.7 2.3 collective-permute-start.6
  347.0 2.3 collective-permute-start.4
  349.3 39.9 %while.5 = (s32[]{:T(128)}, f32[128,2,4,80]{0,3,2,1:T(8,128)}, f32[128,2,4]{0,2,1:T(4,128)S(1)}, f32[128,2,4]{0,2,1:T(4,128)S(1)}, pred[4096]{0:T(1024)(128)(4,1...) while((s32[]{:T(128)}, f32[128,2,4,80]{0,3,2,1:T(8,128)}, ...), condition=%wide.region_4.5_spmd.clone, body=%wide.region_1.4_spmd.clone.sunk | while | flops 174118016 | bytes 10396435 | solution.py:108
  352.1 1.5 fusion.86
  354.7 1.4 fusion.83
  357.1 1.5 fusion.86
  359.7 1.4 fusion.83
  362.1 1.5 fusion.86
  364.6 1.4 fusion.83
  367.1 1.5 fusion.86
  369.6 1.4 fusion.83
  372.0 1.5 fusion.86
  374.6 1.4 fusion.83
  377.0 1.5 fusion.86
  379.6 1.4 fusion.83
  382.0 1.5 fusion.86
  387.0 1.5 fusion.86
  389.2 2.5 collective-permute-start.5
  391.7 3.4 collective-permute-start.7
  396.4 1.6 collective-permute-done.7
  400.2 5.9 %all-to-all-start = ((bf16[128,4,640]{2,0,1:T(8,128)(2,1)}), bf16[128,4,640]{2,0,1:T(8,128)(2,1)}, u32[]{:S(2)}, u32[]{:S(2)}) async-start(bf16[128,4,640]{2,0,1:T(8,128)(2,1)} %concatenate.60), calls=%async_computation | async-start | bytes 1310720 | tf_op jit(solution)/shard_map/all_to_all | solution.py:198
  407.5 5.7 %copy.70 = bf16[2,64,20,640]{3,2,0,1:T(8,128)(2,1)} copy(bf16[2,64,20,640]{3,1,0,2:T(8,128)(2,1)} %bitcast.127) | data formatting | bytes 6553600 | tf_op jit(solution)/shard_map/all_gather | solution.py:33
  413.2 6.1 %reshape.262 = bf16[2560,640]{1,0:T(8,128)(2,1)} reshape(bf16[64,2,20,640]{3,2,1,0:T(8,128)(2,1)} %bitcast.124) | data formatting | bytes 6553600 | tf_op jit(solution)/shard_map/reshape | solution.py:35
  419.6 5.0 %gather_fusion.1 = bf16[1024,160]{1,0:T(8,128)(2,1)} fusion(bf16[160,512]{0,1:T(8,128)(2,1)S(1)} %copy.57, s32[1024]{0:T(1024)S(1)} %fusion.58), kind=kCustom, calls=%fused_computation.1.clone | custom fusion | bytes 659456 | tf_op jit(solution)/shard_map/jit(_take)/gather | solution.py:207
  424.6 5.0 %gather_fusion = bf16[1024,160]{1,0:T(8,128)(2,1)} fusion(bf16[160,512]{0,1:T(8,128)(2,1)S(1)} %copy.55, s32[1024]{0:T(1024)S(1)} %fusion.58), kind=kCustom, calls=%fused_computation.clone | custom fusion | bytes 659456 | tf_op jit(solution)/shard_map/jit(_take)/gather | solution.py:206
  429.6 2.9 bitcast_select_fusion.2
  432.5 1.9 copy.59
  434.5 1.9 copy.60
  436.4 2.2 copy.52
  438.6 2.5 convolution_convert_fusion
  (180 shorter events, 34.3 us)
Async XLA Ops:
  7.2 151.1 %all-gather.15.cloned.1.call-start = ((), (), s32[]{:S(2)}) async-start(), calls=%async_computation.3 | async-start | bytes 3194880 | tf_op jit(solution)/shard_map/all_gather | solution.py:32
  8.7 288.4 %all-gather.17.cloned.1.call-start = ((), (), s32[]{:S(2)}) async-start(), calls=%async_computation.4 | async-start | bytes 1996800 | tf_op jit(solution)/shard_map/all_gather | solution.py:32
  9.5 312.3 %all-gather.11.cloned.1.call-start = ((), (), s32[]{:S(2)}) async-start(), calls=%async_computation.1 | async-start | bytes 7864320 | tf_op jit(solution)/shard_map/all_gather | solution.py:33
  163.1 1.0 copy-start.1
  163.1 2.9 copy-start.2
  163.1 6.4 %copy-start.5 = (s32[32]{0:T(128)S(1)}, s32[32]{0:T(128)}, u32[]{:S(2)}) copy-start(s32[32]{0:T(128)} %param.25) | copy-start | bytes 388
  163.1 8.8 %copy-start.4 = (bf16[2560]{0:T(1024)(128)(2,1)S(1)}, bf16[2560]{0:T(1024)(128)(2,1)}, u32[]{:S(2)}) copy-start(bf16[2560]{0:T(1024)(128)(2,1)} %param.16) | copy-start | bytes 15364
  163.1 8.8 %copy-start.6 = (s32[32]{0:T(128)S(1)}, s32[32]{0:T(128)}, u32[]{:S(2)}) copy-start(s32[32]{0:T(128)} %param.23) | copy-start | bytes 388
  163.1 9.4 %copy-start.7 = (s32[32]{0:T(128)S(1)}, s32[32]{0:T(128)}, u32[]{:S(2)}) copy-start(s32[32]{0:T(128)} %param.24) | copy-start | bytes 388
  163.1 15.3 %copy-start.3 = (bf16[128,640]{1,0:T(8,128)(2,1)S(1)}, bf16[128,640]{1,0:T(8,128)(2,1)}, u32[]{:S(2)}) copy-start(bf16[128,640]{1,0:T(8,128)(2,1)} %param.15) | copy-start | bytes 491524
  163.1 244.4 %all-gather.13.cloned.1.call-start = ((), (), s32[]{:S(2)}) async-start(), calls=%async_computation.2 | async-start | bytes 4915200 | tf_op jit(solution)/shard_map/all_gather | solution.py:33
  164.1 29.0 %collective-permute-start.2 = (bf16[160,1024]{1,0:T(8,128)(2,1)S(1)}, bf16[160,1024]{1,0:T(8,128)(2,1)S(1)}, u32[]{:S(2)}, u32[]{:S(2)}) collective-permute-start(bf16[160,1024]{1,0:T(8,128)(2,1)S(1)} %copy-done.1), channel_id=1, source_target_pairs={{0,4},{4,0},{8,12},{12,8},{16,20},{20,16},{24,28},{28,24},{32,36},... | collective-permute-start | bytes 983048 | tf_op jit(solution)/shard_map/ppermute | solution.py:24
  166.0 27.1 %collective-permute-start = (bf16[160,1024]{1,0:T(8,128)(2,1)S(1)}, bf16[160,1024]{1,0:T(8,128)(2,1)S(1)}, u32[]{:S(2)}, u32[]{:S(2)}) collective-permute-start(bf16[160,1024]{1,0:T(8,128)(2,1)S(1)} %copy-done.2), channel_id=1, source_target_pairs={{0,4},{4,0},{8,12},{12,8},{16,20},{20,16},{24,28},{28,24},{32,36},... | collective-permute-start | bytes 983048 | tf_op jit(solution)/shard_map/ppermute | solution.py:24
  193.3 19.7 %collective-permute-start.1 = (bf16[160,2048]{1,0:T(8,128)(2,1)S(1)}, bf16[160,2048]{1,0:T(8,128)(2,1)S(1)}, u32[]{:S(2)}, u32[]{:S(2)}) collective-permute-start(bf16[160,2048]{1,0:T(8,128)(2,1)S(1)} %pad_maximum_fusion.2), channel_id=1, source_target_pairs={{0,8},{8,0},{4,12},{12,4},{16,24},{24,16},{20,28},{28,20},{32,40},... | collective-permute-start | bytes 1966088 | tf_op jit(solution)/shard_map/ppermute | solution.py:24
  197.5 25.3 %collective-permute-start.3 = (bf16[160,2048]{1,0:T(8,128)(2,1)S(1)}, bf16[160,2048]{1,0:T(8,128)(2,1)S(1)}, u32[]{:S(2)}, u32[]{:S(2)}) collective-permute-start(bf16[160,2048]{1,0:T(8,128)(2,1)S(1)} %pad_maximum_fusion.3), channel_id=1, source_target_pairs={{0,8},{8,0},{4,12},{12,4},{16,24},{24,16},{20,28},{28,20},{32,40},... | collective-permute-start | bytes 1966088 | tf_op jit(solution)/shard_map/ppermute | solution.py:24
  344.7 44.5 %collective-permute-start.6 = (bf16[128,160]{0,1:T(8,128)(2,1)S(1)}, bf16[128,160]{0,1:T(8,128)(2,1)S(1)}, u32[]{:S(2)}, u32[]{:S(2)}) collective-permute-start(bf16[128,160]{0,1:T(8,128)(2,1)S(1)} %slice.49), channel_id=1, source_target_pairs={{0,4},{4,0},{8,12},{12,8},{16,20},{20,16},{24,28},{28,24},{32,36},... | collective-permute-start | bytes 122888 | tf_op jit(solution)/shard_map/ppermute | solution.py:24
  347.0 42.2 %collective-permute-start.4 = (bf16[128,160]{0,1:T(8,128)(2,1)S(1)}, bf16[128,160]{0,1:T(8,128)(2,1)S(1)}, u32[]{:S(2)}, u32[]{:S(2)}) collective-permute-start(bf16[128,160]{0,1:T(8,128)(2,1)S(1)} %bitcast.138), channel_id=1, source_target_pairs={{0,4},{4,0},{8,12},{12,8},{16,20},{20,16},{24,28},{28,24},{32,36},... | collective-permute-start | bytes 122888 | tf_op jit(solution)/shard_map/ppermute | solution.py:24
  351.1 1.0 copy-start.8
  353.6 0.7 copy-start.9
  356.1 1.0 copy-start.8
  358.6 0.7 copy-start.9
  361.1 1.0 copy-start.8
  363.5 0.7 copy-start.9
  366.1 1.0 copy-start.8
  368.5 0.7 copy-start.9
  371.1 1.0 copy-start.8
  373.5 0.7 copy-start.9
  376.1 1.0 copy-start.8
  378.5 0.7 copy-start.9
  381.0 1.0 copy-start.8
  383.5 0.7 copy-start.9
  386.0 1.0 copy-start.8
  388.5 0.7 copy-start.9
  389.2 6.6 %collective-permute-start.5 = (bf16[256,160]{0,1:T(8,128)(2,1)S(1)}, bf16[256,160]{0,1:T(8,128)(2,1)S(1)}, u32[]{:S(2)}, u32[]{:S(2)}) collective-permute-start(bf16[256,160]{0,1:T(8,128)(2,1)S(1)} %pad_maximum_fusion.7), channel_id=1, source_target_pairs={{0,8},{8,0},{4,12},{12,4},{16,24},{24,16},{20,28},{28,20},{32,40},... | collective-permute-start | bytes 245768 | tf_op jit(solution)/shard_map/ppermute | solution.py:24
  391.7 6.3 %collective-permute-start.7 = (bf16[256,160]{0,1:T(8,128)(2,1)S(1)}, bf16[256,160]{0,1:T(8,128)(2,1)S(1)}, u32[]{:S(2)}, u32[]{:S(2)}) collective-permute-start(bf16[256,160]{0,1:T(8,128)(2,1)S(1)} %pad_maximum_fusion.8), channel_id=1, source_target_pairs={{0,8},{8,0},{4,12},{12,4},{16,24},{24,16},{20,28},{28,20},{32,40},... | collective-permute-start | bytes 245768 | tf_op jit(solution)/shard_map/ppermute | solution.py:24
  396.4 2.2 copy-start.10
  400.2 36.2 %all-to-all-start = ((bf16[128,4,640]{2,0,1:T(8,128)(2,1)}), bf16[128,4,640]{2,0,1:T(8,128)(2,1)}, u32[]{:S(2)}, u32[]{:S(2)}) async-start(bf16[128,4,640]{2,0,1:T(8,128)(2,1)} %concatenate.60), calls=%async_computation | async-start | bytes 1310720 | tf_op jit(solution)/shard_map/all_to_all | solution.py:198
  429.6 9.0 %copy-start = (bf16[2560,640]{1,0:T(8,128)(2,1)S(1)}, bf16[2560,640]{1,0:T(8,128)(2,1)}, u32[]{:S(2)}) copy-start(bf16[2560,640]{1,0:T(8,128)(2,1)} %reshape.262) | copy-start | bytes 9830404
Sparse Core Ops, SparseCore 0:
  11.5 146.6 all-gather.14
  161.2 135.8 all-gather.16
  299.2 22.4 all-gather.10
  323.7 24.1 all-gather.12
